TPU v7x, 32 devices: a whole 2x2x4 slice. The times are simulated.
32 devices in a mesh: groups: 2 (over y), ctx: 4 (over z), tm: 2 (over x), tp: 2 (over core).
Axes of the slice: x: 2, y: 2, z: 4, core: 2. Of those that a mesh axis runs over, the one named last changes fastest.
Arguments:
- tokens: bfloat16 [256, 8, 1024], P(('groups', 'tm'), 'ctx'), parts along dimension 0, may hold values from -6 to 6
- norm_gain: float32 [1024], replicated, may hold values from 0.1 to 1.9
- block_mask: int32 [4, 4, 4], P(('groups', 'tm'), 'ctx'), parts along dimension 0, may hold values from 0 to 1, as said below
- w_query: bfloat16 [1024, 1024], P('tm', 'tp'), may hold values from -1.25 to 1.25
- w_key: bfloat16 [1024, 1024], P('tm', 'tp'), may hold values from -1.25 to 1.25
- w_value: bfloat16 [1024, 1024], P('tm', 'tp'), may hold values from -0.1875 to 0.1875
- w_out: bfloat16 [1024, 1024], P('tp', 'tm'), may hold values from -0.1875 to 0.1875
- w_up: bfloat16 [1024, 2048], P('tm', 'tp'), may hold values from -0.1875 to 0.1875
- w_down: bfloat16 [2048, 1024], P('tp', 'tm'), may hold values from -0.125 to 0.125
- conv_weight: float32 [5, 1024], P(None, 'tp'), may hold values from -2.5 to 2.5
Outputs:
- denoised: bfloat16 [256, 8, 1024], P(('groups', 'tm'), 'ctx', 'tp'), parts along dimension 0
There are 2 independent parts, one for each index of `groups`. A program takes and returns all parts, laid end to end along the dimension named above; an argument that names none is the same for every part. Nothing has to cross between parts.
Inputs may be any that keep to these rules, and one draw needn't show every extreme that they name: block_mask[w, i, i] is 1 for every window w and block i.
All inputs are finite; a program needn't handle non-finite values.
Results may differ from a plain program's by a relative error of at most 0.0076.
Values may be sent and summed in bfloat16 or wider, within the bound.
A program may use at most 64 MiB of HBM per device.

v0:
```python
import jax
import jax.numpy as jnp
from jax import lax
from jax.sharding import PartitionSpec as P

HEAD_DIM = 64
KERNEL = 5


def from_behind(value, axis, steps):
    count = lax.axis_size(axis)
    first, last = (max(0, -steps), min(count, count - steps))
    return lax.ppermute(value, axis, [(source, source + steps) for source in range(first, last)])


def rms_norm(tokens, norm_gain):
    values = tokens.astype(jnp.float32)
    square = jnp.mean(values * values, axis=-1, keepdims=True)
    return (values * lax.rsqrt(square + 1e-05) * norm_gain).astype(jnp.bfloat16)


def on_device(
    tokens, norm_gain, block_mask, w_query, w_key, w_value, w_out, w_up, w_down, conv_weight
):
    frames_here, dancers_here, width = tokens.shape
    rows_here = frames_here * dancers_here
    normed_grid = rms_norm(tokens, norm_gain)
    normed = normed_grid.reshape(rows_here, width)
    pieces = (
        lax.all_gather(w_query, "tm", axis=0, tiled=True),
        lax.all_gather(w_key, "tm", axis=0, tiled=True),
        lax.all_gather(w_value, "tm", axis=0, tiled=True),
        lax.all_gather(w_up, "tm", axis=0, tiled=True),
    )
    query_sum, key_sum, value_sum, hidden = tuple(
        (jnp.dot(normed, piece_one, preferred_element_type=jnp.float32) for piece_one in pieces)
    )
    local_heads = query_sum.shape[1] // HEAD_DIM
    queries = query_sum.astype(jnp.bfloat16).reshape(rows_here, local_heads, HEAD_DIM)
    key_grid = key_sum.astype(jnp.bfloat16).reshape(
        frames_here, dancers_here, local_heads * HEAD_DIM
    )
    value_grid = value_sum.astype(jnp.bfloat16).reshape(
        frames_here, dancers_here, local_heads * HEAD_DIM
    )
    mask_row = block_mask[0, 0].astype(jnp.float32)
    cycle_blocks = mask_row.shape[0]
    key_piece = lax.all_gather(key_grid, "ctx", axis=1, tiled=True)
    value_piece = lax.all_gather(value_grid, "ctx", axis=1, tiled=True)
    count = key_piece.shape[1]
    block_ids = jnp.arange(count) // dancers_here
    picker = (block_ids[:, None] == jnp.arange(cycle_blocks)[None, :]).astype(jnp.float32)
    allowed_dancers = jnp.dot(picker, mask_row)
    peak_old = jnp.full((local_heads, rows_here), -1e30, jnp.float32)
    key_rows = key_piece.reshape(frames_here * count, local_heads, HEAD_DIM)
    value_rows = value_piece.reshape(frames_here * count, local_heads, HEAD_DIM)
    allowed = jnp.tile(allowed_dancers, frames_here)
    scores = (
        jnp.einsum("qhd,khd->hqk", queries, key_rows, preferred_element_type=jnp.float32) * 0.125
    )
    scores = jnp.where(allowed[None, None, :] > 0, scores, -1e30)
    peak_new = jnp.maximum(peak_old, jnp.max(scores, axis=-1))
    expo = jnp.exp(scores - peak_new[:, :, None]) * allowed[None, None, :]
    total_new = jnp.sum(expo, axis=-1)
    probs = expo.astype(jnp.bfloat16)
    mixed_new = jnp.einsum("hqk,khd->hqd", probs, value_rows, preferred_element_type=jnp.float32)
    attended = (
        (mixed_new / total_new[:, :, None])
        .transpose(1, 0, 2)
        .reshape(rows_here, local_heads * HEAD_DIM)
        .astype(jnp.bfloat16)
    )
    activated = jax.nn.gelu(hidden, approximate=True).astype(jnp.bfloat16)
    out_full, down_full = (
        lax.all_gather(w_out, "tm", axis=1, tiled=True),
        lax.all_gather(w_down, "tm", axis=1, tiled=True),
    )
    branches = jnp.dot(attended, out_full, preferred_element_type=jnp.float32)
    branches = branches + jnp.dot(activated, down_full, preferred_element_type=jnp.float32)
    mine = lax.psum_scatter(
        branches.astype(jnp.bfloat16), "tp", scatter_dimension=1, tiled=True
    ).astype(jnp.float32)
    features_here = mine.shape[1]
    first_feature = lax.axis_index("tp") * features_here
    normed_cols = lax.dynamic_slice_in_dim(normed_grid, first_feature, features_here, 2)
    padded = jnp.pad(normed_cols.astype(jnp.float32), ((4, 4), (0, 0), (0, 0)))
    extended = jnp.zeros((frames_here + 4, dancers_here, features_here), jnp.float32)
    for offset in range(KERNEL):
        extended = extended + conv_weight[offset] * padded[offset : offset + frames_here + 4]
    convolved = extended[2 : frames_here + 2]
    from_before = from_behind(extended[frames_here + 2 :], "tm", 1)
    from_after = from_behind(extended[0:2], "tm", -1)
    convolved = convolved.at[0:2].add(from_before)
    convolved = convolved.at[frames_here - 2 :].add(from_after)
    token_cols = lax.dynamic_slice_in_dim(tokens, first_feature, features_here, 2).astype(
        jnp.float32
    )
    result = token_cols + mine.reshape(frames_here, dancers_here, features_here) + convolved
    return result.astype(jnp.bfloat16)


def solution(mesh):
    placed = (
        P(("groups", "tm"), "ctx", None),
        P(),
        P(("groups", "tm"), "ctx", None),
        P("tm", "tp"),
        P("tm", "tp"),
        P("tm", "tp"),
        P("tp", "tm"),
        P("tm", "tp"),
        P("tp", "tm"),
        P(None, "tp"),
    )
    return jax.shard_map(
        on_device,
        mesh=mesh,
        in_specs=placed,
        out_specs=P(("groups", "tm"), "ctx", "tp"),
        check_vma=False,
    )
```

profile of v0, /device:TPU:0, one launch (start us, length us, event | category | flops | bytes accessed | tf_op | source)
XLA Modules:
  0.0 189.4 jit_solution(12623946930418223822)
XLA Ops:
  6.5 0.7 all-gather.7.cloned.1.call-update
  7.3 0.7 all-gather.9.cloned.1.call-update
  8.1 0.7 all-gather.11.cloned.1.call-update
  8.8 0.5 all-gather.17.cloned.1.call-update
  9.4 0.5 all-gather.15.cloned.1.call-update
  10.0 0.5 all-gather.13.cloned.1.call-update
  10.6 0.3 fusion.15
  12.0 1.0 fusion.26
  13.0 19.9 %all-gather.7.cloned.1.call-done = bf16[1024,512]{1,0:T(8,128)(2,1)} async-done(((bf16[512,512]{1,0:T(8,128)(2,1)}), bf16[1024,512]{1,0:T(8,128)(2,1)}) %all-gather.7.cloned.1.call-update) | async-done | bytes 1048592 | tf_op jit(solution)/shard_map/all_gather | solution.py:30
  32.9 1.5 convolution_convert_fusion.2
  34.6 21.2 %all-gather.9.cloned.1.call-done = bf16[1024,512]{1,0:T(8,128)(2,1)} async-done(((bf16[512,512]{1,0:T(8,128)(2,1)}), bf16[1024,512]{1,0:T(8,128)(2,1)}) %all-gather.9.cloned.1.call-update) | async-done | bytes 1048592 | tf_op jit(solution)/shard_map/all_gather | solution.py:31
  55.8 1.5 convolution_convert_fusion.1
  57.4 15.5 %all_gather.26 = bf16[64,8,512]{2,0,1:T(8,128)(2,1)S(1)} all-gather(bf16[64,2,512]{2,0,1:T(8,128)(2,1)S(1)} %copy.35), channel_id=1, replica_groups=mesh['groups'=2,'ctx'=4,'tm'=2,'tp'=2] {'ctx'}, dimensions={1}, use_global_device_ids=true | all-gather | bytes 655360 | tf_op jit(solution)/shard_map/all_gather | solution.py:48
  73.1 0.5 reshape.130
  73.7 5.0 %all-gather.11.cloned.1.call-done = bf16[1024,512]{1,0:T(8,128)(2,1)} async-done(((bf16[512,512]{1,0:T(8,128)(2,1)}), bf16[1024,512]{1,0:T(8,128)(2,1)}) %all-gather.11.cloned.1.call-update) | async-done | bytes 1048592 | tf_op jit(solution)/shard_map/all_gather | solution.py:32
  78.6 1.5 convolution_convert_fusion
  80.3 0.6 fusion
  80.9 15.5 %all_gather.28 = bf16[64,8,512]{2,0,1:T(8,128)(2,1)S(1)} all-gather(bf16[64,2,512]{2,0,1:T(8,128)(2,1)S(1)} %copy.38), channel_id=1, replica_groups=mesh['groups'=2,'ctx'=4,'tm'=2,'tp'=2] {'ctx'}, dimensions={1}, use_global_device_ids=true | all-gather | bytes 655360 | tf_op jit(solution)/shard_map/all_gather | solution.py:49
  96.6 1.5 reshape.132
  98.2 0.6 fusion.1
  98.8 0.6 copy-done.3
  99.4 0.9 fusion.5
  100.2 12.9 %all-gather.17.cloned.1.call-done = bf16[1024,1024]{1,0:T(8,128)(2,1)} async-done(((bf16[1024,512]{1,0:T(8,128)(2,1)}), bf16[1024,1024]{1,0:T(8,128)(2,1)}) %all-gather.17.cloned.1.call-update) | async-done | bytes 2097168 | tf_op jit(solution)/shard_map/all_gather | solution.py:76
  113.2 34.5 %all-gather.15.cloned.1.call-done = bf16[1024,1024]{1,0:T(8,128)(2,1)} async-done(((bf16[512,1024]{1,0:T(8,128)(2,1)}), bf16[1024,1024]{1,0:T(8,128)(2,1)}) %all-gather.15.cloned.1.call-update) | async-done | bytes 2097168 | tf_op jit(solution)/shard_map/all_gather | solution.py:33
  147.7 3.1 %fusion.30 = f32[128,1024]{1,0:T(8,128)S(1)} fusion(bf16[1024,1024]{1,0:T(8,128)(2,1)} %all-gather.17.cloned.1.call-done, bf16[128,1024]{1,0:T(8,128)(2,1)S(1)} %reshape.127, bf16[1024,1024]{1,0:T(8,128)(2,1)} %all-gather.15.cloned.1.call-done), kind=kOutput, calls=%fused_computation.45 | convolution fusion | flops 538050560 | bytes 4980736 | tf_op jit(solution)/shard_map/dot_general | solution.py:79
  150.8 19.6 %all-gather.13.cloned.1.call-done = bf16[512,1024]{1,0:T(8,128)(2,1)} async-done(((bf16[512,512]{1,0:T(8,128)(2,1)}), bf16[512,1024]{1,0:T(8,128)(2,1)}) %all-gather.13.cloned.1.call-update) | async-done | bytes 1048592 | tf_op jit(solution)/shard_map/all_gather | solution.py:75
  170.4 2.3 %fusion.3 = bf16[128,1024]{1,0:T(8,128)(2,1)} fusion(f32[128,1024]{1,0:T(8,128)S(1)} %fusion.30, bf16[128,512]{0,1:T(8,128)(2,1)S(1)} %bitcast.34, bf16[512,1024]{1,0:T(8,128)(2,1)} %all-gather.13.cloned.1.call-done), kind=kOutput, calls=%fused_computation.6 | convolution fusion | flops 134479872 | bytes 1966080 | tf_op jit(solution)/shard_map/dot_general | solution.py:78
  172.7 2.3 %collective-permute-start = (f32[2,2,512]{2,1,0:T(2,128)S(1)}, f32[2,2,512]{2,1,0:T(2,128)S(1)}, u32[]{:S(2)}, u32[]{:S(2)}) collective-permute-start(f32[2,2,512]{2,1,0:T(2,128)S(1)} %get-tuple-element.30), channel_id=1, source_target_pairs={{0,2},{1,3},{4,6},{5,7},{8,10},{9,11},{12,14},{13,15},{16,18},{17,... | collective-permute-start | bytes 24584 | tf_op jit(solution)/shard_map/ppermute | solution.py:13
  175.0 1.3 collective-permute-start.1
  176.3 4.2 %collective-permute-done.1 = f32[2,2,512]{2,1,0:T(2,128)S(1)} collective-permute-done((f32[2,2,512]{2,1,0:T(2,128)S(1)}, f32[2,2,512]{2,1,0:T(2,128)S(1)}, u32[]{:S(2)}, u32[]{:S(2)}) %collective-permute-start.1) | collective-permute-done | bytes 8224 | tf_op jit(solution)/shard_map/ppermute | solution.py:13
  180.6 1.1 reshape.136
  181.7 0.8 add_convert_fusion
  (47 shorter events, 2.3 us)
Async XLA Ops:
  6.5 4.0 %copy-start = (bf16[64,2,1024]{2,1,0:T(2,128)(2,1)S(1)}, bf16[64,2,1024]{2,1,0:T(2,128)(2,1)}, u32[]{:S(2)}) copy-start(bf16[64,2,1024]{2,1,0:T(2,128)(2,1)} %param.14) | copy-start | bytes 786436
  6.5 26.4 %all-gather.7.cloned.1.call-start = ((), (), s32[]{:S(2)}) async-start(), calls=%async_computation.1 | async-start | bytes 1572864 | tf_op jit(solution)/shard_map/all_gather | solution.py:30
  7.3 3.7 %copy-start.5 = (f32[1024]{0:T(1024)S(1)}, f32[1024]{0:T(1024)}, u32[]{:S(2)}) copy-start(f32[1024]{0:T(1024)} %param.15) | copy-start | bytes 12292
  7.3 48.5 %all-gather.9.cloned.1.call-start = ((), (), s32[]{:S(2)}) async-start(), calls=%async_computation.2 | async-start | bytes 1572864 | tf_op jit(solution)/shard_map/all_gather | solution.py:31
  8.0 70.6 %all-gather.11.cloned.1.call-start = ((), (), s32[]{:S(2)}) async-start(), calls=%async_computation.3 | async-start | bytes 1572864 | tf_op jit(solution)/shard_map/all_gather | solution.py:32
  8.8 104.4 %all-gather.17.cloned.1.call-start = ((), (), s32[]{:S(2)}) async-start(), calls=%async_computation.6 | async-start | bytes 3145728 | tf_op jit(solution)/shard_map/all_gather | solution.py:76
  9.3 2.3 %copy-start.4 = (f32[5,512]{1,0:T(8,128)S(1)}, f32[5,512]{1,0:T(8,128)}, u32[]{:S(2)}) copy-start(f32[5,512]{1,0:T(8,128)} %param.23) | copy-start | bytes 30724
  9.3 2.3 %copy-start.6 = (s32[1,1,4]{2,1,0:T(1,128)S(1)}, s32[1,1,4]{2,1,0:T(1,128)}, u32[]{:S(2)}) copy-start(s32[1,1,4]{2,1,0:T(1,128)} %param.16) | copy-start | bytes 52
  9.3 138.3 %all-gather.15.cloned.1.call-start = ((), (), s32[]{:S(2)}) async-start(), calls=%async_computation.5 | async-start | bytes 3145728 | tf_op jit(solution)/shard_map/all_gather | solution.py:33
  9.9 160.5 %all-gather.13.cloned.1.call-start = ((), (), s32[]{:S(2)}) async-start(), calls=%async_computation.4 | async-start | bytes 1572864 | tf_op jit(solution)/shard_map/all_gather | solution.py:75
  10.5 170.1 %reduce-scatter.2.cloned.1.call-start = ((), (), s32[]{:S(2)}) async-start(), calls=%async_computation.7 | async-start | bytes 393216 | tf_op jit(solution)/shard_map/reduce_scatter | solution.py:80
  98.1 1.2 copy-start.3
  150.7 21.9 %copy-start.2 = (f32[68,2,512]{2,1,0:T(2,128)S(1)}, f32[68,2,512]{2,1,0:T(2,128)}, u32[]{:S(2)}) copy-start(f32[68,2,512]{2,1,0:T(2,128)} %fusion.26) | copy-start | bytes 835588
  150.8 25.5 %slice-start = ((f32[68,2,512]{2,1,0:T(2,128)}), f32[64,2,512]{2,1,0:T(2,128)S(1)}, s32[]{:S(2)}) async-start(f32[68,2,512]{2,1,0:T(2,128)} %fusion.26), calls=%async_computation.8 | async-start | bytes 524288 | tf_op jit(solution)/shard_map/slice | solution.py:90
  150.8 30.9 %copy-start.1 = (bf16[64,2,1024]{2,1,0:T(2,128)(2,1)S(1)}, bf16[64,2,1024]{2,1,0:T(2,128)(2,1)}, u32[]{:S(2)}) copy-start(bf16[64,2,1024]{2,1,0:T(2,128)(2,1)} %param.14) | copy-start | bytes 786436
  172.7 3.6 %collective-permute-start = (f32[2,2,512]{2,1,0:T(2,128)S(1)}, f32[2,2,512]{2,1,0:T(2,128)S(1)}, u32[]{:S(2)}, u32[]{:S(2)}) collective-permute-start(f32[2,2,512]{2,1,0:T(2,128)S(1)} %get-tuple-element.30), channel_id=1, source_target_pairs={{0,2},{1,3},{4,6},{5,7},{8,10},{9,11},{12,14},{13,15},{16,18},{17,... | collective-permute-start | bytes 24584 | tf_op jit(solution)/shard_map/ppermute | solution.py:13
  175.0 5.5 %collective-permute-start.1 = (f32[2,2,512]{2,1,0:T(2,128)S(1)}, f32[2,2,512]{2,1,0:T(2,128)S(1)}, u32[]{:S(2)}, u32[]{:S(2)}) collective-permute-start(f32[2,2,512]{2,1,0:T(2,128)S(1)} %get-tuple-element.29), channel_id=1, source_target_pairs={{2,0},{3,1},{6,4},{7,5},{10,8},{11,9},{14,12},{15,13},{18,16},{19,... | collective-permute-start | bytes 24584 | tf_op jit(solution)/shard_map/ppermute | solution.py:13
Sparse Core Ops, SparseCore 0:
  8.9 23.9 all-gather.6
  34.5 21.2 all-gather.8
  57.3 21.2 all-gather.10
  80.0 33.0 all-gather.16
  114.5 33.0 all-gather.14
  149.1 21.2 all-gather.12
  172.8 7.7 reduce-scatter.1
where the time goes:
time: 190 us; the launch traced here: 189 us
  waiting for transfers between devices  121 us (64%)
  blocking collectives  30.9 us (16%)
  between operations  13.8 us (7%)
  matrix products  11.6 us (6%)
  local copies, waits for them, and re-layouts  4.94 us (3%)
  starting transfers between devices  3.77 us (2%)
  other arithmetic  3.36 us (2%)
    all_gather x1, waiting for transfers between devices, on_device(): lax.all_gather(w_up, 'tm', axis=0, tiled=True)  34.5 us
    all_gather x1, waiting for transfers between devices, on_device(): lax.all_gather(w_key, 'tm', axis=0, tiled=True)  21.2 us
    all_gather x1, waiting for transfers between devices, on_device(): lax.all_gather(w_query, 'tm', axis=0, tiled=True)  19.9 us
    all_gather x1, waiting for transfers between devices, on_device(): lax.all_gather(w_out, 'tm', axis=1, tiled=True)  19.6 us
    all_gather x1, blocking collectives, on_device(): key_piece = lax.all_gather(key_grid, 'ctx', axis=1, tiled=True)  15.5 us
    all_gather x1, blocking collectives, on_device(): value_piece = lax.all_gather(value_grid, 'ctx', axis=1, tiled=True)  15.5 us
    all_gather x1, waiting for transfers between devices, on_device(): lax.all_gather(w_down, 'tm', axis=1, tiled=True)  12.9 us
    all_gather x1, waiting for transfers between devices, on_device(): lax.all_gather(w_value, 'tm', axis=0, tiled=True)  4.95 us
  transfers between devices with their start and end apart: 9, of which 8 were waited for; matrix products, arithmetic and copies ran while one was open for 8% of the time, Pallas kernels for 0%

commit v1 on v0

--- a/solution.py
+++ b/solution.py
@@ -5,6 +5,13 @@
 
 HEAD_DIM = 64
 KERNEL = 5
+
+
+def side_direct(message):
+    return jnp.concatenate(
+        lax.all_to_all(jnp.stack(tuple((message for _ in range(lax.axis_size("tm"))))), "tm", 0, 0),
+        axis=0,
+    )
 
 
 def from_behind(value, axis, steps):
@@ -27,7 +34,7 @@
     normed_grid = rms_norm(tokens, norm_gain)
     normed = normed_grid.reshape(rows_here, width)
     pieces = (
-        lax.all_gather(w_query, "tm", axis=0, tiled=True),
+        side_direct(w_query),
         lax.all_gather(w_key, "tm", axis=0, tiled=True),
         lax.all_gather(w_value, "tm", axis=0, tiled=True),
         lax.all_gather(w_up, "tm", axis=0, tiled=True),

time: 190 us -> 176 us (0.926)
  waiting for transfers between devices: 121 us -> 102 us
  starting transfers between devices: 3.77 us -> 8.06 us
    all_to_all x0 -> x1, waiting for transfers between devices: none -> 20 us  [side_direct(): lax.all_to_all(jnp.stack(tuple((message for _ in range(lax.axis_size('tm'...]
    all_gather x1 -> x0, waiting for transfers between devices: 19.9 us -> none  [on_device(): lax.all_gather(w_query, 'tm', axis=0, tiled=True)]
    all_gather x1, waiting for transfers between devices: 21.2 us -> 2.41 us  [on_device(): lax.all_gather(w_key, 'tm', axis=0, tiled=True)]
    all_to_all x0 -> x1, starting transfers between devices: none -> 4.37 us  [side_direct(): lax.all_to_all(jnp.stack(tuple((message for _ in range(lax.axis_size('tm'...]
  transfers between devices with their start and end apart: 9 -> 9, of which waited for: 8 -> 8; matrix products, arithmetic and copies ran while one was open for 8% -> 9% of each run, Pallas kernels for 0% -> 0%
where the time goes in v1:
time: 176 us; the launch traced here: 175 us
  waiting for transfers between devices  102 us (58%)
  blocking collectives  31.7 us (18%)
  between operations  13.7 us (8%)
  matrix products  10.4 us (6%)
  starting transfers between devices  8.06 us (5%)
  local copies, waits for them, and re-layouts  4.94 us (3%)
  other arithmetic  4.51 us (3%)
    all_gather x1, waiting for transfers between devices, on_device(): lax.all_gather(w_up, 'tm', axis=0, tiled=True)  34.5 us
    all_to_all x1, waiting for transfers between devices, side_direct(): lax.all_to_all(jnp.stack(tuple((message for _ in range(lax.axis_size('tm'...  20 us
    all_gather x1, waiting for transfers between devices, on_device(): lax.all_gather(w_out, 'tm', axis=1, tiled=True)  19.6 us
    all_gather x1, blocking collectives, on_device(): key_piece = lax.all_gather(key_grid, 'ctx', axis=1, tiled=True)  16.2 us
    all_gather x1, blocking collectives, on_device(): value_piece = lax.all_gather(value_grid, 'ctx', axis=1, tiled=True)  15.5 us
    all_gather x1, waiting for transfers between devices, on_device(): lax.all_gather(w_down, 'tm', axis=1, tiled=True)  13.1 us
    all_gather x1, waiting for transfers between devices, on_device(): lax.all_gather(w_value, 'tm', axis=0, tiled=True)  4.73 us
    all_to_all x1, starting transfers between devices, side_direct(): lax.all_to_all(jnp.stack(tuple((message for _ in range(lax.axis_size('tm'...  4.37 us
  transfers between devices with their start and end apart: 9, of which 8 were waited for; matrix products, arithmetic and copies ran while one was open for 9% of the time, Pallas kernels for 0%

profile of v1, /device:TPU:0, one launch (start us, length us, event | category | flops | bytes accessed | tf_op | source)
XLA Modules:
  0.0 175.1 jit_solution(6878374878553459795)
XLA Ops:
  6.5 0.7 all-gather.6.cloned.1.call-update
  7.3 0.7 all-gather.8.cloned.1.call-update
  8.1 0.7 all-gather.14.cloned.1.call-update
  8.8 0.5 all-gather.12.cloned.1.call-update
  9.4 1.1 pad_maximum_fusion
  10.5 4.4 %all-to-all-start = ((bf16[2,512,512]{2,1,0:T(8,128)(2,1)}), bf16[2,512,512]{2,1,0:T(8,128)(2,1)S(1)}, u32[]{:S(2)}, u32[]{:S(2)}) async-start(bf16[2,512,512]{2,1,0:T(8,128)(2,1)} %pad_maximum_fusion), calls=%async_computation | async-start | bytes 2097152 | tf_op jit(solution)/shard_map/all_to_all | solution.py:12
  14.9 0.6 all-gather.10.cloned.1.call-update
  15.5 0.3 fusion.15
  16.9 1.0 fusion.26
  18.0 20.0 %all-to-all-done = bf16[2,512,512]{2,1,0:T(8,128)(2,1)S(1)} async-done(((bf16[2,512,512]{2,1,0:T(8,128)(2,1)}), bf16[2,512,512]{2,1,0:T(8,128)(2,1)S(1)}, u32[]{:S(2)}, u32[]{:S(2)}) %all-to-all-start) | async-done | bytes 1048608 | tf_op jit(solution)/shard_map/all_to_all | solution.py:12
  38.4 2.4 %all-gather.6.cloned.1.call-done = bf16[1024,512]{1,0:T(8,128)(2,1)} async-done(((bf16[512,512]{1,0:T(8,128)(2,1)}), bf16[1024,512]{1,0:T(8,128)(2,1)}) %all-gather.6.cloned.1.call-update) | async-done | bytes 1048592 | tf_op jit(solution)/shard_map/all_gather | solution.py:38
  40.8 1.5 convolution_convert_fusion.1
  42.4 16.2 %all_gather.22 = bf16[64,8,512]{2,0,1:T(8,128)(2,1)S(1)} all-gather(bf16[64,2,512]{2,0,1:T(8,128)(2,1)S(1)} %copy.35), channel_id=1, replica_groups=mesh['groups'=2,'ctx'=4,'tm'=2,'tp'=2] {'ctx'}, dimensions={1}, use_global_device_ids=true | all-gather | bytes 655360 | tf_op jit(solution)/shard_map/all_gather | solution.py:55
  58.9 0.5 reshape.134
  59.5 4.7 %all-gather.8.cloned.1.call-done = bf16[1024,512]{1,0:T(8,128)(2,1)} async-done(((bf16[512,512]{1,0:T(8,128)(2,1)}), bf16[1024,512]{1,0:T(8,128)(2,1)}) %all-gather.8.cloned.1.call-update) | async-done | bytes 1048592 | tf_op jit(solution)/shard_map/all_gather | solution.py:39
  64.2 1.5 convolution_convert_fusion
  65.8 0.6 fusion
  66.4 15.5 %all_gather.24 = bf16[64,8,512]{2,0,1:T(8,128)(2,1)S(1)} all-gather(bf16[64,2,512]{2,0,1:T(8,128)(2,1)S(1)} %copy.38), channel_id=1, replica_groups=mesh['groups'=2,'ctx'=4,'tm'=2,'tp'=2] {'ctx'}, dimensions={1}, use_global_device_ids=true | all-gather | bytes 655360 | tf_op jit(solution)/shard_map/all_gather | solution.py:56
  82.2 1.5 reshape.136
  83.7 0.6 fusion.1
  84.4 0.6 copy-done.3
  84.9 0.9 fusion.5
  85.8 13.1 %all-gather.14.cloned.1.call-done = bf16[1024,1024]{1,0:T(8,128)(2,1)} async-done(((bf16[1024,512]{1,0:T(8,128)(2,1)}), bf16[1024,1024]{1,0:T(8,128)(2,1)}) %all-gather.14.cloned.1.call-update) | async-done | bytes 2097168 | tf_op jit(solution)/shard_map/all_gather | solution.py:83
  98.9 34.5 %all-gather.12.cloned.1.call-done = bf16[1024,1024]{1,0:T(8,128)(2,1)} async-done(((bf16[512,1024]{1,0:T(8,128)(2,1)}), bf16[1024,1024]{1,0:T(8,128)(2,1)}) %all-gather.12.cloned.1.call-update) | async-done | bytes 2097168 | tf_op jit(solution)/shard_map/all_gather | solution.py:40
  133.4 3.1 %fusion.30 = f32[128,1024]{1,0:T(8,128)S(1)} fusion(bf16[1024,1024]{1,0:T(8,128)(2,1)} %all-gather.14.cloned.1.call-done, bf16[128,1024]{1,0:T(8,128)(2,1)S(1)} %reshape.130, bf16[1024,1024]{1,0:T(8,128)(2,1)} %all-gather.12.cloned.1.call-done), kind=kOutput, calls=%fused_computation.46 | convolution fusion | flops 538050560 | bytes 4980736 | tf_op jit(solution)/shard_map/dot_general | solution.py:86
  136.5 19.6 %all-gather.10.cloned.1.call-done = bf16[512,1024]{1,0:T(8,128)(2,1)} async-done(((bf16[512,512]{1,0:T(8,128)(2,1)}), bf16[512,1024]{1,0:T(8,128)(2,1)}) %all-gather.10.cloned.1.call-update) | async-done | bytes 1048592 | tf_op jit(solution)/shard_map/all_gather | solution.py:82
  156.1 2.3 %fusion.3 = bf16[128,1024]{1,0:T(8,128)(2,1)} fusion(f32[128,1024]{1,0:T(8,128)S(1)} %fusion.30, bf16[128,512]{0,1:T(8,128)(2,1)S(1)} %bitcast.38, bf16[512,1024]{1,0:T(8,128)(2,1)} %all-gather.10.cloned.1.call-done), kind=kOutput, calls=%fused_computation.6 | convolution fusion | flops 134479872 | bytes 1966080 | tf_op jit(solution)/shard_map/dot_general | solution.py:85
  158.4 2.3 %collective-permute-start = (f32[2,2,512]{2,1,0:T(2,128)S(1)}, f32[2,2,512]{2,1,0:T(2,128)S(1)}, u32[]{:S(2)}, u32[]{:S(2)}) collective-permute-start(f32[2,2,512]{2,1,0:T(2,128)S(1)} %get-tuple-element.30), channel_id=1, source_target_pairs={{0,2},{1,3},{4,6},{5,7},{8,10},{9,11},{12,14},{13,15},{16,18},{17,... | collective-permute-start | bytes 24584 | tf_op jit(solution)/shard_map/ppermute | solution.py:20
  160.7 1.3 collective-permute-start.1
  162.0 4.2 %collective-permute-done.1 = f32[2,2,512]{2,1,0:T(2,128)S(1)} collective-permute-done((f32[2,2,512]{2,1,0:T(2,128)S(1)}, f32[2,2,512]{2,1,0:T(2,128)S(1)}, u32[]{:S(2)}, u32[]{:S(2)}) %collective-permute-start.1) | collective-permute-done | bytes 8224 | tf_op jit(solution)/shard_map/ppermute | solution.py:20
  166.3 1.1 reshape.140
  167.4 0.8 add_convert_fusion
  (49 shorter events, 2.5 us)
Async XLA Ops:
  6.5 2.8 %copy-start.4 = (bf16[512,512]{1,0:T(8,128)(2,1)S(1)}, bf16[512,512]{1,0:T(8,128)(2,1)}, u32[]{:S(2)}) copy-start(bf16[512,512]{1,0:T(8,128)(2,1)} %param.17) | copy-start | bytes 1572868
  6.5 34.2 %all-gather.6.cloned.1.call-start = ((), (), s32[]{:S(2)}) async-start(), calls=%async_computation.2 | async-start | bytes 1572864 | tf_op jit(solution)/shard_map/all_gather | solution.py:38
  7.3 57.0 %all-gather.8.cloned.1.call-start = ((), (), s32[]{:S(2)}) async-start(), calls=%async_computation.3 | async-start | bytes 1572864 | tf_op jit(solution)/shard_map/all_gather | solution.py:39
  8.0 90.9 %all-gather.14.cloned.1.call-start = ((), (), s32[]{:S(2)}) async-start(), calls=%async_computation.6 | async-start | bytes 3145728 | tf_op jit(solution)/shard_map/all_gather | solution.py:83
  8.7 124.7 %all-gather.12.cloned.1.call-start = ((), (), s32[]{:S(2)}) async-start(), calls=%async_computation.5 | async-start | bytes 3145728 | tf_op jit(solution)/shard_map/all_gather | solution.py:40
  9.3 6.2 %copy-start = (bf16[64,2,1024]{2,1,0:T(2,128)(2,1)S(1)}, bf16[64,2,1024]{2,1,0:T(2,128)(2,1)}, u32[]{:S(2)}) copy-start(bf16[64,2,1024]{2,1,0:T(2,128)(2,1)} %param.14) | copy-start | bytes 786436
  9.3 6.5 %copy-start.6 = (f32[1024]{0:T(1024)S(1)}, f32[1024]{0:T(1024)}, u32[]{:S(2)}) copy-start(f32[1024]{0:T(1024)} %param.15) | copy-start | bytes 12292
  10.5 6.0 %copy-start.7 = (s32[1,1,4]{2,1,0:T(1,128)S(1)}, s32[1,1,4]{2,1,0:T(1,128)}, u32[]{:S(2)}) copy-start(s32[1,1,4]{2,1,0:T(1,128)} %param.16) | copy-start | bytes 52
  10.5 6.4 %copy-start.5 = (f32[5,512]{1,0:T(8,128)S(1)}, f32[5,512]{1,0:T(8,128)}, u32[]{:S(2)}) copy-start(f32[5,512]{1,0:T(8,128)} %param.23) | copy-start | bytes 30724
  10.5 27.4 %all-to-all-start = ((bf16[2,512,512]{2,1,0:T(8,128)(2,1)}), bf16[2,512,512]{2,1,0:T(8,128)(2,1)S(1)}, u32[]{:S(2)}, u32[]{:S(2)}) async-start(bf16[2,512,512]{2,1,0:T(8,128)(2,1)} %pad_maximum_fusion), calls=%async_computation | async-start | bytes 2097152 | tf_op jit(solution)/shard_map/all_to_all | solution.py:12
  14.9 141.2 %all-gather.10.cloned.1.call-start = ((), (), s32[]{:S(2)}) async-start(), calls=%async_computation.4 | async-start | bytes 1572864 | tf_op jit(solution)/shard_map/all_gather | solution.py:82
  15.4 150.9 %reduce-scatter.2.cloned.1.call-start = ((), (), s32[]{:S(2)}) async-start(), calls=%async_computation.7 | async-start | bytes 393216 | tf_op jit(solution)/shard_map/reduce_scatter | solution.py:87
  83.7 1.2 copy-start.3
  136.5 21.9 %copy-start.2 = (f32[68,2,512]{2,1,0:T(2,128)S(1)}, f32[68,2,512]{2,1,0:T(2,128)}, u32[]{:S(2)}) copy-start(f32[68,2,512]{2,1,0:T(2,128)} %fusion.26) | copy-start | bytes 835588
  136.5 25.5 %slice-start = ((f32[68,2,512]{2,1,0:T(2,128)}), f32[64,2,512]{2,1,0:T(2,128)S(1)}, s32[]{:S(2)}) async-start(f32[68,2,512]{2,1,0:T(2,128)} %fusion.26), calls=%async_computation.8 | async-start | bytes 524288 | tf_op jit(solution)/shard_map/slice | solution.py:97
  136.5 30.9 %copy-start.1 = (bf16[64,2,1024]{2,1,0:T(2,128)(2,1)S(1)}, bf16[64,2,1024]{2,1,0:T(2,128)(2,1)}, u32[]{:S(2)}) copy-start(bf16[64,2,1024]{2,1,0:T(2,128)(2,1)} %param.14) | copy-start | bytes 786436
  158.4 3.6 %collective-permute-start = (f32[2,2,512]{2,1,0:T(2,128)S(1)}, f32[2,2,512]{2,1,0:T(2,128)S(1)}, u32[]{:S(2)}, u32[]{:S(2)}) collective-permute-start(f32[2,2,512]{2,1,0:T(2,128)S(1)} %get-tuple-element.30), channel_id=1, source_target_pairs={{0,2},{1,3},{4,6},{5,7},{8,10},{9,11},{12,14},{13,15},{16,18},{17,... | collective-permute-start | bytes 24584 | tf_op jit(solution)/shard_map/ppermute | solution.py:20
  160.7 5.5 %collective-permute-start.1 = (f32[2,2,512]{2,1,0:T(2,128)S(1)}, f32[2,2,512]{2,1,0:T(2,128)S(1)}, u32[]{:S(2)}, u32[]{:S(2)}) collective-permute-start(f32[2,2,512]{2,1,0:T(2,128)S(1)} %get-tuple-element.29), channel_id=1, source_target_pairs={{2,0},{3,1},{6,4},{7,5},{10,8},{11,9},{14,12},{15,13},{18,16},{19,... | collective-permute-start | bytes 24584 | tf_op jit(solution)/shard_map/ppermute | solution.py:20
Sparse Core Ops, SparseCore 0:
  8.9 31.8 all-gather.5
  42.3 21.8 all-gather.7
  65.8 33.0 all-gather.13
  100.3 33.0 all-gather.11
  134.8 21.2 all-gather.9
  158.5 7.7 reduce-scatter.1
